TPU v7x, 128 devices: a whole 4x4x4 slice. The times are simulated.
128 devices in a mesh: gx: 16 (over x_hi, z, core), gy: 8 (over x_lo, y).
Axes of the slice: x: 4 (x_hi: 2, x_lo: 2; x = x_hi * 2 + x_lo), y: 4, z: 4, core: 2. Of those that a mesh axis runs over, the one named last changes fastest.
Arguments:
- populations: float32 [19, 256, 128, 128], P(None, 'gx', 'gy')
- panels: bfloat16 [64, 200, 128], P(None, None, ('gx', 'gy')), may hold values from -0.59765625 to 0.59765625
- modal_vel: bfloat16 [64, 2, 200], replicated, may hold values from -0.4375 to 0.4375
- marker_x: int32 [16, 8, 512], P('gx', 'gy'), may hold values from 0 to 15
- marker_y: int32 [16, 8, 512], P('gx', 'gy'), may hold values from 0 to 15
- marker_z: int32 [16, 8, 512], P('gx', 'gy'), may hold values from 0 to 127
- marker_riser: int32 [16, 8, 512], P('gx', 'gy'), may hold values from 0 to 63
Outputs:
- next_populations: float32 [19, 256, 128, 128], P(None, 'gx', 'gy')
- marker_force: float32 [16, 8, 3, 512], P('gx', 'gy')
- force_field: float32 [3, 256, 128, 128], P(None, 'gx', 'gy')
All inputs are finite; a program needn't handle non-finite values.
Results may differ from a plain program's by a relative error of at most 0.0008.
Values may be sent and summed in bfloat16 or wider, within the bound.
No kernel may reach another device: no remote copies, remote signals or barrier semaphores. Data moves between devices by JAX's collectives and lax.ppermute only.
A program may use at most 128 MiB of HBM per device.

v0:
```python
import jax
import jax.numpy as jnp
from jax import lax
from jax.sharding import PartitionSpec as P

VELOCITY = (
    (0, 0, 0),
    (1, 0, 0),
    (-1, 0, 0),
    (0, 1, 0),
    (0, -1, 0),
    (0, 0, 1),
    (0, 0, -1),
    (1, 1, 0),
    (-1, -1, 0),
    (1, -1, 0),
    (-1, 1, 0),
    (1, 0, 1),
    (-1, 0, -1),
    (1, 0, -1),
    (-1, 0, 1),
    (0, 1, 1),
    (0, -1, -1),
    (0, 1, -1),
    (0, -1, 1),
)
WEIGHT = (1.0 / 3.0,) + (1.0 / 18.0,) * 6 + (1.0 / 36.0,) * 12
KERNEL = (0.25, 0.5, 0.25)
RELAX = 0.8


def extended(shard, sides, width):
    for axis, dim in sides:
        devices, length = (lax.axis_size(axis), shard.shape[dim])
        up = [(i, (i + 1) % devices) for i in range(devices)]
        down = [(j, i) for i, j in up]
        last = lax.slice_in_dim(shard, length - width, length, axis=dim)
        first = lax.slice_in_dim(shard, 0, width, axis=dim)
        before = lax.ppermute(last, axis, up)
        after = lax.ppermute(first, axis, down)
        shard = jnp.concatenate([before, shard, after], axis=dim)
    return shard


def along(vector, direction):
    total = jnp.zeros_like(vector[0])
    for axis_pos in range(3):
        if direction[axis_pos] == 1:
            total = total + vector[axis_pos]
        elif direction[axis_pos] == -1:
            total = total - vector[axis_pos]
    return total


def moments(fields):
    density = fields[0]
    for index in range(1, 19):
        density = density + fields[index]
    rows = []
    for axis_pos in range(3):
        total = jnp.zeros_like(density)
        for index in range(19):
            if VELOCITY[index][axis_pos] == 1:
                total = total + fields[index]
            elif VELOCITY[index][axis_pos] == -1:
                total = total - fields[index]
        rows.append(total)
    return (density, jnp.stack(rows))


def collide(fields, density, momentum, field):
    velocity = (momentum + 0.5 * field) / density
    square = velocity[0] * velocity[0] + velocity[1] * velocity[1] + velocity[2] * velocity[2]
    work = velocity[0] * field[0] + velocity[1] * field[1] + velocity[2] * field[2]
    outputs = []
    for index in range(19):
        proj_u = along(velocity, VELOCITY[index])
        proj_f = along(field, VELOCITY[index])
        equil = (
            WEIGHT[index] * density * (1.0 + 3.0 * proj_u + 4.5 * proj_u * proj_u - 1.5 * square)
        )
        source = (
            (1.0 - 0.5 / RELAX) * WEIGHT[index] * (3.0 * (proj_f - work) + 9.0 * proj_u * proj_f)
        )
        outputs.append(fields[index] - (fields[index] - equil) / RELAX + source)
    return jnp.stack(outputs)


def kernel_rows(position, span):
    count = position.shape[0]
    column = lax.broadcasted_iota(jnp.int32, (count, span), 1)
    total = jnp.zeros((count, span), jnp.float32)
    for shift_a in range(3):
        total = total + KERNEL[shift_a] * (column == position[:, None] + shift_a).astype(
            jnp.float32
        )
    return total


def on_device(populations, panels, modal_vel, marker_x, marker_y, marker_z, marker_riser):
    cells_x = populations.shape[1]
    cells_y = populations.shape[2]
    depth = populations.shape[3]
    widened = extended(populations, (("gx", 1), ("gy", 2)), 2)
    read_cycle = jnp.stack(
        [
            jnp.roll(
                widened[
                    i,
                    1 - VELOCITY[i][0] : 3 - VELOCITY[i][0] + cells_x,
                    1 - VELOCITY[i][1] : 3 - VELOCITY[i][1] + cells_y,
                ],
                VELOCITY[i][2],
                axis=2,
            )
            for i in range(19)
        ]
    )
    density_cycle, momentum_cycle = moments(read_cycle)
    fluid_cycle = momentum_cycle / density_cycle
    read = read_cycle[:, 1 : cells_x + 1, 1 : cells_y + 1]
    density = density_cycle[1 : cells_x + 1, 1 : cells_y + 1]
    momentum = momentum_cycle[:, 1 : cells_x + 1, 1 : cells_y + 1]
    targets = jnp.einsum(
        "rcm,rmz->rcz",
        modal_vel,
        lax.all_gather(panels, ("gx", "gy"), axis=2, tiled=True),
        preferred_element_type=jnp.float32,
    )
    pos_x = marker_x[0, 0]
    pos_y = marker_y[0, 0]
    pos_z = marker_z[0, 0]
    riser = marker_riser[0, 0]
    count = pos_x.shape[0]
    span_x = cells_x + 2
    span_y = cells_y + 2
    plane_size = span_x * span_y
    highest = lax.Precision.HIGHEST
    weight_x = kernel_rows(pos_x, span_x)
    weight_y = kernel_rows(pos_y, span_y)
    plane = (weight_x[:, :, None] * weight_y[:, None, :]).reshape(count, plane_size).T
    depth_hot = (lax.broadcasted_iota(jnp.int32, (count, depth), 1) == pos_z[:, None]).astype(
        jnp.float32
    )
    contract_depth = (((1,), (1,)), ((), ()))
    picked = lax.dot_general(
        fluid_cycle.reshape(3 * plane_size, depth),
        depth_hot,
        contract_depth,
        precision=highest,
        preferred_element_type=jnp.float32,
    )
    sampled = jnp.sum(picked.reshape(3, plane_size, count) * plane[None], axis=1)
    risers = targets.shape[0]
    target_cols = lax.dot_general(
        targets.reshape(risers * 2, depth),
        depth_hot,
        contract_depth,
        precision=highest,
        preferred_element_type=jnp.float32,
    ).reshape(risers, 2, count)
    riser_hot = (lax.broadcasted_iota(jnp.int32, (risers, count), 0) == riser[None, :]).astype(
        jnp.float32
    )
    chosen = jnp.sum(target_cols * riser_hot[:, None, :], axis=0)
    wanted = jnp.concatenate([chosen, jnp.zeros((1, count), jnp.float32)], axis=0)
    force = 2.0 * (wanted - sampled)
    spread = (force[:, None, :] * plane[None]).reshape(3 * plane_size, count)
    region = jnp.dot(
        spread, depth_hot, precision=highest, preferred_element_type=jnp.float32
    ).reshape(3, span_x, span_y, depth)
    rim_x = jnp.stack([region[:, 0], region[:, cells_x + 1]], axis=1)
    got_x = extended(rim_x, (("gx", 1),), 1)
    region = region.at[:, 1].add(got_x[:, 0]).at[:, cells_x].add(got_x[:, 3])
    inner = region[:, 1 : cells_x + 1]
    rim_y = jnp.stack([inner[:, :, 0], inner[:, :, cells_y + 1]], axis=2)
    got_y = extended(rim_y, (("gy", 2),), 1)
    inner = inner.at[:, :, 1].add(got_y[:, :, 0]).at[:, :, cells_y].add(got_y[:, :, 3])
    field = inner[:, :, 1 : cells_y + 1]
    next_populations = collide(read, density, momentum, field)
    return (next_populations, force[None, None], field)


def solution(mesh):
    in_specs = (
        P(None, "gx", "gy", None),
        P(None, None, ("gx", "gy")),
        P(),
        P("gx", "gy", None),
        P("gx", "gy", None),
        P("gx", "gy", None),
        P("gx", "gy", None),
    )
    out_specs = (P(None, "gx", "gy", None), P("gx", "gy", None, None), P(None, "gx", "gy", None))
    return jax.shard_map(
        on_device, mesh=mesh, in_specs=in_specs, out_specs=out_specs, check_vma=False
    )
```

profile of v0, /device:TPU:97, one launch (start us, length us, event | category | flops | bytes accessed | tf_op | source)
XLA Modules:
  0.0 365.4 jit_solution(12806877301452564051)
XLA Ops:
  7.2 1.8 fusion.221
  9.1 1.9 collective-permute-start
  13.1 1.7 collective-permute-done
  14.9 2.1 constant_dynamic-update-slice_fusion.1
  16.9 4.3 %collective-permute-done.1 = f32[19,2,16,128]{3,2,1,0:T(8,128)} collective-permute-done((f32[19,2,16,128]{3,2,1,0:T(8,128)}, f32[19,2,16,128]{3,2,1,0:T(8,128)}, u32[]{:S(2)}, u32[]{:S(2)}) %collective-permute-start.1) | collective-permute-done | bytes 311328 | tf_op jit(solution)/shard_map/ppermute | solution.py:40
  21.2 1.0 constant_dynamic-update-slice_fusion
  22.3 1.2 fusion.220
  23.5 2.8 collective-permute-start.3
  26.2 1.0 broadcast_multiply_fusion
  27.2 2.1 mul.602
  29.3 2.1 mul.608
  32.1 2.2 collective-permute-done.3
  34.3 4.3 %collective-permute-done.2 = f32[19,20,2,128]{3,2,1,0:T(2,128)} collective-permute-done((f32[19,20,2,128]{3,2,1,0:T(2,128)}, f32[19,20,2,128]{3,2,1,0:T(2,128)}, u32[]{:S(2)}, u32[]{:S(2)}) %collective-permute-start.2) | collective-permute-done | bytes 389152 | tf_op jit(solution)/shard_map/ppermute | solution.py:39
  38.6 2.0 maximum_bitcast_fusion.8
  41.2 0.9 slice_bitcast_fusion.23
  42.1 1.9 concatenate.407
  44.8 2.1 slice_bitcast_fusion.21
  47.0 1.8 concatenate.411
  48.7 1.7 slice_bitcast_fusion.25
  51.3 1.8 slice_reduce_fusion.9
  53.1 1.5 slice_reduce_fusion.7
  54.7 2.7 slice_reduce_fusion.5
  57.4 2.2 fusion.20
  59.7 1.0 maximum_bitcast_fusion.2
  61.9 0.9 slice_bitcast_fusion.17
  62.8 1.0 slice_reduce_fusion
  63.8 0.9 slice_bitcast_fusion.16
  64.8 2.0 add_subtract_fusion
  68.4 1.3 add_add_fusion
  69.8 1.6 div.77
  71.4 0.9 concatenate.415
  73.1 0.9 concatenate.408
  74.0 0.9 concatenate.409
  74.9 1.8 concatenate.413
  76.7 0.9 concatenate.412
  78.5 0.9 concatenate.417
  79.4 0.9 concatenate.422
  80.2 1.8 concatenate.418
  82.0 1.8 concatenate.421
  83.8 1.8 concatenate.419
  85.5 1.8 concatenate.424
  87.3 0.9 concatenate.420
  88.2 0.9 concatenate.423
  89.1 0.9 concatenate.405
  90.0 2.9 add_subtract_fusion.1
  92.9 1.8 stack.113
  94.6 1.8 stack.114
  96.4 3.8 %subtract_add_fusion = f32[1,18,18,128]{3,2,1,0:T(8,128)} fusion(f32[1,18,18,1]{3,2,1,0:T(8,128)} %copy-done.54, f32[1,18,18,127]{3,2,1,0:T(8,128)} %get-tuple-element.154, f32[1,18,18,127]{3,2,1,0:T(8,128)} %get-tuple-element.127, f32[1,18,18,1]{3,2,1,0:T(8,128)} %copy-done.52, f32[1,18,18,127]{3,2,1,0:T(8,128)} %copy-done.36, ...), kind=kLoop, calls=%fused_computation.72 | loop fusion | flops 787968 | bytes 1824768 | tf_op jit(solution)/shard_map/add | solution.py:64
  106.5 3.8 %fusion.27 = f32[1,324,128]{2,0,1:T(1,128)S(1)} fusion(f32[1,324,1]{2,0,1:T(1,128)S(1)} %copy-done.87, f32[1,324,127]{2,0,1:T(1,128)S(1)} %copy-done.85, f32[1,324,1]{2,0,1:T(1,128)S(1)} %copy-done.82, f32[1,324,127]{2,0,1:T(1,128)S(1)} %copy-done.84, f32[1,324,127]{2,0,1:T(1,128)S(1)} %copy-done.86, f32[1,324,1]{2,0,1:T(1,128)S(1)} %copy-done.88, ...), kind=kLoop, calls=%fused_computation.113 | loop fusion | flops 787968 | bytes 1824768 | tf_op jit(solution)/shard_map/add | solution.py:64
  110.9 1.1 multiply_reduce_fusion
  112.5 204.5 %all-gather.2.cloned.1.call-done = bf16[64,200,128]{1,0,2:T(8,128)(2,1)} async-done(((bf16[64,200,1]{1,0,2:T(8,128)(2,1)}), bf16[64,200,128]{1,0,2:T(8,128)(2,1)}) %all-gather.2.cloned.1.call-update) | async-done | bytes 3276816 | tf_op jit(solution)/shard_map/all_gather | solution.py:127
  317.0 4.6 %fusion = f32[64,2,128]{2,1,0:T(2,128)S(1)} fusion(bf16[64,2,200]{2,1,0:T(2,128)(2,1)S(1)} %copy-done, bf16[64,200,128]{1,0,2:T(8,128)(2,1)} %all-gather.2.cloned.1.call-done), kind=kOutput, calls=%fused_computation | convolution fusion | flops 6553600 | bytes 3393536 | tf_op jit(solution)/shard_map/rcm,rmz->rcz/dot_general | solution.py:124
  322.1 1.5 fusion.2
  323.7 2.7 collective-permute-start.4
  328.4 6.7 %collective-permute-done.5 = f32[3,1,18,128]{3,2,1,0:T(8,128)S(1)} collective-permute-done((f32[3,1,18,128]{3,2,1,0:T(8,128)S(1)}, f32[3,1,18,128]{3,2,1,0:T(8,128)S(1)}, u32[]{:S(2)}, u32[]{:S(2)}) %collective-permute-start.5) | collective-permute-done | bytes 27680 | tf_op jit(solution)/shard_map/ppermute | solution.py:40
  337.9 3.0 collective-permute-start.7
  340.9 1.7 scatter-add.16
  342.6 1.0 slice_add_fusion.2
  343.6 1.7 scatter-add.19
  345.3 2.3 fusion.9
  347.6 1.3 bitcast_dynamic-update-slice_fusion
  350.7 0.9 fusion.63
  354.5 0.9 fusion.117
  357.1 1.4 copy-done.107
  (275 shorter events, 27.8 us)
Async XLA Ops:
  7.2 309.9 %copy-start = (bf16[64,2,200]{2,1,0:T(2,128)(2,1)S(1)}, bf16[64,2,200]{2,1,0:T(2,128)(2,1)}, u32[]{:S(2)}) copy-start(bf16[64,2,200]{2,1,0:T(2,128)(2,1)} %param.17) | copy-start | bytes 153604
  7.2 309.8 %all-gather.2.cloned.1.call-start = ((), (), s32[]{:S(2)}) async-start(), calls=%async_computation | async-start | bytes 4227072 | tf_op jit(solution)/shard_map/all_gather | solution.py:127
  9.1 5.8 %collective-permute-start = (f32[19,2,16,128]{3,2,1,0:T(8,128)S(1)}, f32[19,2,16,128]{3,2,1,0:T(8,128)S(1)}, u32[]{:S(2)}, u32[]{:S(2)}) collective-permute-start(f32[19,2,16,128]{3,2,1,0:T(8,128)S(1)} %get-tuple-element.76), channel_id=1, source_target_pairs={{0,8},{8,16},{16,24},{24,32},{32,40},{40,48},{48,56},{56,64},{64,7... | collective-permute-start | bytes 933896 | tf_op jit(solution)/shard_map/ppermute | solution.py:39
  11.0 10.3 %collective-permute-start.1 = (f32[19,2,16,128]{3,2,1,0:T(8,128)}, f32[19,2,16,128]{3,2,1,0:T(8,128)}, u32[]{:S(2)}, u32[]{:S(2)}) collective-permute-start(f32[19,2,16,128]{3,2,1,0:T(8,128)} %get-tuple-element.75), channel_id=1, source_target_pairs={{8,0},{16,8},{24,16},{32,24},{40,32},{48,40},{56,48},{64,56},{72,6... | collective-permute-start | bytes 933896 | tf_op jit(solution)/shard_map/ppermute | solution.py:40
  22.2 9.2 %copy-start.108 = (s32[1,1,512]{2,1,0:T(1,128)S(1)}, s32[1,1,512]{2,1,0:T(1,128)}, u32[]{:S(2)}) copy-start(s32[1,1,512]{2,1,0:T(1,128)} %param.21) | copy-start | bytes 6148
  23.5 10.9 %collective-permute-start.3 = (f32[19,20,2,128]{3,2,1,0:T(2,128)}, f32[19,20,2,128]{3,2,1,0:T(2,128)}, u32[]{:S(2)}, u32[]{:S(2)}) collective-permute-start(f32[19,20,2,128]{3,2,1,0:T(2,128)} %get-tuple-element.74), channel_id=1, source_target_pairs={{1,0},{2,1},{3,2},{4,3},{5,4},{6,5},{7,6},{0,7},{9,8},{10,9},{11,1... | collective-permute-start | bytes 1167368 | tf_op jit(solution)/shard_map/ppermute | solution.py:40
  26.2 12.3 %collective-permute-start.2 = (f32[19,20,2,128]{3,2,1,0:T(2,128)}, f32[19,20,2,128]{3,2,1,0:T(2,128)}, u32[]{:S(2)}, u32[]{:S(2)}) collective-permute-start(f32[19,20,2,128]{3,2,1,0:T(2,128)} %get-tuple-element.73), channel_id=1, source_target_pairs={{0,1},{1,2},{2,3},{3,4},{4,5},{5,6},{6,7},{7,0},{8,9},{9,10},{10,1... | collective-permute-start | bytes 1167368 | tf_op jit(solution)/shard_map/ppermute | solution.py:39
  42.1 6.6 %copy-start.23 = (f32[18,18,127]{2,1,0:T(8,128)}, f32[18,18,127]{2,1,0:T(8,128)S(1)}, u32[]{:S(2)}) copy-start(f32[18,18,127]{2,1,0:T(8,128)S(1)} %get-tuple-element.112) | copy-start | bytes 493780
  50.4 9.2 %copy-start.21 = (f32[18,18,127]{2,1,0:T(8,128)}, f32[18,18,127]{2,1,0:T(8,128)S(1)}, u32[]{:S(2)}) copy-start(f32[18,18,127]{2,1,0:T(8,128)S(1)} %get-tuple-element.128) | copy-start | bytes 493780
  51.3 6.1 %copy-start.24 = (f32[18,18,127]{2,1,0:T(8,128)S(1)}, f32[18,18,127]{2,1,0:T(8,128)}, u32[]{:S(2)}) copy-start(f32[18,18,127]{2,1,0:T(8,128)} %copy-done.23) | copy-start | bytes 493780
  51.3 6.1 %copy-start.26 = (f32[18,18,127]{2,1,0:T(8,128)S(1)}, f32[18,18,127]{2,1,0:T(8,128)}, u32[]{:S(2)}) copy-start(f32[18,18,127]{2,1,0:T(8,128)} %get-tuple-element.153) | copy-start | bytes 493780
  51.3 6.1 %copy-start.28 = (f32[18,18,127]{2,1,0:T(8,128)S(1)}, f32[18,18,127]{2,1,0:T(8,128)}, u32[]{:S(2)}) copy-start(f32[18,18,127]{2,1,0:T(8,128)} %get-tuple-element.151) | copy-start | bytes 493780
  53.1 14.6 %copy-start.52 = (f32[1,18,18,1]{3,2,1,0:T(8,128)}, f32[1,18,18,1]{3,2,1,0:T(8,128)S(1)}, u32[]{:S(2)}) copy-start(f32[1,18,18,1]{3,2,1,0:T(8,128)S(1)} %get-tuple-element.82) | copy-start | bytes 3892
  54.6 13.0 %copy-start.18 = (f32[1,18,18,1]{3,2,1,0:T(8,128)}, f32[1,18,18,1]{3,2,1,0:T(8,128)S(1)}, u32[]{:S(2)}) copy-start(f32[1,18,18,1]{3,2,1,0:T(8,128)S(1)} %get-tuple-element.88) | copy-start | bytes 3892
  54.6 13.0 %copy-start.54 = (f32[1,18,18,1]{3,2,1,0:T(8,128)}, f32[1,18,18,1]{3,2,1,0:T(8,128)S(1)}, u32[]{:S(2)}) copy-start(f32[1,18,18,1]{3,2,1,0:T(8,128)S(1)} %get-tuple-element.145) | copy-start | bytes 3892
  57.3 10.4 %copy-start.19 = (f32[1,18,18,1]{3,2,1,0:T(8,128)}, f32[1,18,18,1]{3,2,1,0:T(8,128)S(1)}, u32[]{:S(2)}) copy-start(f32[1,18,18,1]{3,2,1,0:T(8,128)S(1)} %get-tuple-element.94) | copy-start | bytes 3892
  57.3 10.4 %copy-start.20 = (f32[1,18,18,1]{3,2,1,0:T(8,128)}, f32[1,18,18,1]{3,2,1,0:T(8,128)S(1)}, u32[]{:S(2)}) copy-start(f32[1,18,18,1]{3,2,1,0:T(8,128)S(1)} %get-tuple-element.142) | copy-start | bytes 3892
  59.6 8.1 %copy-start.38 = (f32[1,18,18,128]{3,2,1,0:T(8,128)}, f32[1,18,18,128]{3,2,1,0:T(8,128)S(1)}, u32[]{:S(2)}) copy-start(f32[1,18,18,128]{3,2,1,0:T(8,128)S(1)} %get-tuple-element.58) | copy-start | bytes 497668
  59.6 8.1 %copy-start.39 = (f32[1,18,18,128]{3,2,1,0:T(8,128)}, f32[1,18,18,128]{3,2,1,0:T(8,128)S(1)}, u32[]{:S(2)}) copy-start(f32[1,18,18,128]{3,2,1,0:T(8,128)S(1)} %get-tuple-element.59) | copy-start | bytes 497668
  59.7 8.1 %copy-start.40 = (f32[1,18,18,128]{3,2,1,0:T(8,128)}, f32[1,18,18,128]{3,2,1,0:T(8,128)S(1)}, u32[]{:S(2)}) copy-start(f32[1,18,18,128]{3,2,1,0:T(8,128)S(1)} %get-tuple-element.60) | copy-start | bytes 497668
  59.7 8.1 %copy-start.41 = (f32[1,18,18,128]{3,2,1,0:T(8,128)}, f32[1,18,18,128]{3,2,1,0:T(8,128)S(1)}, u32[]{:S(2)}) copy-start(f32[1,18,18,128]{3,2,1,0:T(8,128)S(1)} %get-tuple-element.61) | copy-start | bytes 497668
  61.9 5.9 %copy-start.30 = (f32[1,18,18,1]{3,2,1,0:T(8,128)}, f32[1,18,18,1]{3,2,1,0:T(8,128)S(1)}, u32[]{:S(2)}) copy-start(f32[1,18,18,1]{3,2,1,0:T(8,128)S(1)} %get-tuple-element.106) | copy-start | bytes 3892
  61.9 5.9 %copy-start.31 = (f32[1,18,18,1]{3,2,1,0:T(8,128)}, f32[1,18,18,1]{3,2,1,0:T(8,128)S(1)}, u32[]{:S(2)}) copy-start(f32[1,18,18,1]{3,2,1,0:T(8,128)S(1)} %get-tuple-element.139) | copy-start | bytes 3892
  68.4 8.3 %copy-start.104 = (f32[18,18]{1,0:T(8,128)S(1)}, f32[18,18]{1,0:T(8,128)}, u32[]{:S(2)}) copy-start(f32[18,18]{1,0:T(8,128)} %get-tuple-element.143) | copy-start | bytes 3892
  68.4 9.2 %copy-start.103 = (f32[18,18]{1,0:T(8,128)S(1)}, f32[18,18]{1,0:T(8,128)}, u32[]{:S(2)}) copy-start(f32[18,18]{1,0:T(8,128)} %get-tuple-element.93) | copy-start | bytes 3892
  69.8 19.3 %copy-start.105 = (f32[18,18]{1,0:T(8,128)S(1)}, f32[18,18]{1,0:T(8,128)}, u32[]{:S(2)}) copy-start(f32[18,18]{1,0:T(8,128)} %get-tuple-element.81) | copy-start | bytes 3892
  96.4 5.7 %copy-start.25 = (f32[18,18,127]{2,1,0:T(8,128)S(1)}, f32[18,18,127]{2,1,0:T(8,128)}, u32[]{:S(2)}) copy-start(f32[18,18,127]{2,1,0:T(8,128)} %copy-done.23) | copy-start | bytes 493780
  96.4 5.7 %copy-start.58 = (f32[18,18,1]{2,1,0:T(8,128)S(1)}, f32[18,18,1]{2,1,0:T(8,128)}, u32[]{:S(2)}) copy-start(f32[18,18,1]{2,1,0:T(8,128)} %copy-done.57) | copy-start | bytes 3892
  96.4 6.6 %copy-start.29 = (f32[18,18,127]{2,1,0:T(8,128)S(1)}, f32[18,18,127]{2,1,0:T(8,128)}, u32[]{:S(2)}) copy-start(f32[18,18,127]{2,1,0:T(8,128)} %get-tuple-element.151) | copy-start | bytes 493780
  96.4 6.5 %copy-start.62 = (f32[18,18,1]{2,1,0:T(8,128)S(1)}, f32[18,18,1]{2,1,0:T(8,128)}, u32[]{:S(2)}) copy-start(f32[18,18,1]{2,1,0:T(8,128)} %copy-done.61) | copy-start | bytes 3892
  96.4 7.4 %copy-start.5 = (f32[18,18,127]{2,1,0:T(8,128)S(1)}, f32[18,18,127]{2,1,0:T(8,128)}, u32[]{:S(2)}) copy-start(f32[18,18,127]{2,1,0:T(8,128)} %get-tuple-element.116) | copy-start | bytes 493780
  96.4 7.4 %copy-start.47 = (f32[18,18,1]{2,1,0:T(8,128)S(1)}, f32[18,18,1]{2,1,0:T(8,128)}, u32[]{:S(2)}) copy-start(f32[18,18,1]{2,1,0:T(8,128)} %get-tuple-element.95) | copy-start | bytes 3892
  100.3 6.0 %copy-start.70 = (f32[1,324,127]{2,0,1:T(1,128)S(1)}, f32[1,324,127]{2,0,1:T(1,128)}, u32[]{:S(2)}) copy-start(f32[1,324,127]{2,0,1:T(1,128)} %concatenate.407) | copy-start | bytes 493780
  100.3 6.0 %copy-start.71 = (f32[1,324,127]{2,0,1:T(1,128)S(1)}, f32[1,324,127]{2,0,1:T(1,128)}, u32[]{:S(2)}) copy-start(f32[1,324,127]{2,0,1:T(1,128)} %concatenate.410) | copy-start | bytes 493780
  100.3 5.9 %copy-start.72 = (f32[1,324,127]{2,0,1:T(1,128)S(1)}, f32[1,324,127]{2,0,1:T(1,128)}, u32[]{:S(2)}) copy-start(f32[1,324,127]{2,0,1:T(1,128)} %concatenate.411) | copy-start | bytes 493780
  100.3 5.9 %copy-start.73 = (f32[1,324,127]{2,0,1:T(1,128)S(1)}, f32[1,324,127]{2,0,1:T(1,128)}, u32[]{:S(2)}) copy-start(f32[1,324,127]{2,0,1:T(1,128)} %concatenate.406) | copy-start | bytes 493780
  100.3 5.9 %copy-start.74 = (f32[1,324,1]{2,0,1:T(1,128)S(1)}, f32[1,324,1]{2,0,1:T(1,128)}, u32[]{:S(2)}) copy-start(f32[1,324,1]{2,0,1:T(1,128)} %concatenate.415) | copy-start | bytes 3892
  100.4 5.9 %copy-start.75 = (f32[1,324,127]{2,0,1:T(1,128)S(1)}, f32[1,324,127]{2,0,1:T(1,128)}, u32[]{:S(2)}) copy-start(f32[1,324,127]{2,0,1:T(1,128)} %concatenate.416) | copy-start | bytes 493780
  100.4 5.9 %copy-start.76 = (f32[1,324,1]{2,0,1:T(1,128)S(1)}, f32[1,324,1]{2,0,1:T(1,128)}, u32[]{:S(2)}) copy-start(f32[1,324,1]{2,0,1:T(1,128)} %concatenate.408) | copy-start | bytes 3892
  100.4 5.9 %copy-start.77 = (f32[1,324,1]{2,0,1:T(1,128)S(1)}, f32[1,324,1]{2,0,1:T(1,128)}, u32[]{:S(2)}) copy-start(f32[1,324,1]{2,0,1:T(1,128)} %concatenate.409) | copy-start | bytes 3892
  100.4 5.9 %copy-start.78 = (f32[1,324,127]{2,0,1:T(1,128)S(1)}, f32[1,324,127]{2,0,1:T(1,128)}, u32[]{:S(2)}) copy-start(f32[1,324,127]{2,0,1:T(1,128)} %concatenate.413) | copy-start | bytes 493780
  100.4 5.9 %copy-start.79 = (f32[1,324,1]{2,0,1:T(1,128)S(1)}, f32[1,324,1]{2,0,1:T(1,128)}, u32[]{:S(2)}) copy-start(f32[1,324,1]{2,0,1:T(1,128)} %concatenate.412) | copy-start | bytes 3892
  100.4 5.9 %copy-start.80 = (f32[1,324,1]{2,0,1:T(1,128)S(1)}, f32[1,324,1]{2,0,1:T(1,128)}, u32[]{:S(2)}) copy-start(f32[1,324,1]{2,0,1:T(1,128)} %concatenate.414) | copy-start | bytes 3892
  100.4 5.9 %copy-start.81 = (f32[1,324,1]{2,0,1:T(1,128)S(1)}, f32[1,324,1]{2,0,1:T(1,128)}, u32[]{:S(2)}) copy-start(f32[1,324,1]{2,0,1:T(1,128)} %concatenate.417) | copy-start | bytes 3892
  100.4 5.9 %copy-start.82 = (f32[1,324,1]{2,0,1:T(1,128)S(1)}, f32[1,324,1]{2,0,1:T(1,128)}, u32[]{:S(2)}) copy-start(f32[1,324,1]{2,0,1:T(1,128)} %concatenate.422) | copy-start | bytes 3892
  100.4 5.9 %copy-start.83 = (f32[1,324,127]{2,0,1:T(1,128)S(1)}, f32[1,324,127]{2,0,1:T(1,128)}, u32[]{:S(2)}) copy-start(f32[1,324,127]{2,0,1:T(1,128)} %concatenate.418) | copy-start | bytes 493780
  100.4 5.9 %copy-start.84 = (f32[1,324,127]{2,0,1:T(1,128)S(1)}, f32[1,324,127]{2,0,1:T(1,128)}, u32[]{:S(2)}) copy-start(f32[1,324,127]{2,0,1:T(1,128)} %concatenate.421) | copy-start | bytes 493780
  100.5 5.9 %copy-start.85 = (f32[1,324,127]{2,0,1:T(1,128)S(1)}, f32[1,324,127]{2,0,1:T(1,128)}, u32[]{:S(2)}) copy-start(f32[1,324,127]{2,0,1:T(1,128)} %concatenate.419) | copy-start | bytes 493780
  100.5 5.9 %copy-start.86 = (f32[1,324,127]{2,0,1:T(1,128)S(1)}, f32[1,324,127]{2,0,1:T(1,128)}, u32[]{:S(2)}) copy-start(f32[1,324,127]{2,0,1:T(1,128)} %concatenate.424) | copy-start | bytes 493780
  100.5 5.9 %copy-start.87 = (f32[1,324,1]{2,0,1:T(1,128)S(1)}, f32[1,324,1]{2,0,1:T(1,128)}, u32[]{:S(2)}) copy-start(f32[1,324,1]{2,0,1:T(1,128)} %concatenate.420) | copy-start | bytes 3892
  104.6 5.8 %copy-start.69 = (f32[324,128]{1,0:T(8,128)S(1)}, f32[324,128]{1,0:T(8,128)}, u32[]{:S(2)}) copy-start(f32[324,128]{1,0:T(8,128)} %div.77) | copy-start | bytes 497668
  104.6 5.8 %copy-start.90 = (f32[1,324,128]{2,0,1:T(1,128)S(1)}, f32[1,324,128]{2,0,1:T(1,128)}, u32[]{:S(2)}) copy-start(f32[1,324,128]{2,0,1:T(1,128)} %stack.113) | copy-start | bytes 497668
  104.6 5.8 %copy-start.91 = (f32[1,324,128]{2,0,1:T(1,128)S(1)}, f32[1,324,128]{2,0,1:T(1,128)}, u32[]{:S(2)}) copy-start(f32[1,324,128]{2,0,1:T(1,128)} %stack.114) | copy-start | bytes 497668
  106.5 5.6 %copy-start.6 = (f32[18,18,127]{2,1,0:T(8,128)S(1)}, f32[18,18,127]{2,1,0:T(8,128)}, u32[]{:S(2)}) copy-start(f32[18,18,127]{2,1,0:T(8,128)} %get-tuple-element.126) | copy-start | bytes 493780
  112.5 215.0 %copy-start.9 = (f32[18,18,127]{2,1,0:T(8,128)S(1)}, f32[18,18,127]{2,1,0:T(8,128)}, u32[]{:S(2)}) copy-start(f32[18,18,127]{2,1,0:T(8,128)} %get-tuple-element.124) | copy-start | bytes 493780
  317.0 9.3 %copy-start.11 = (f32[18,18,127]{2,1,0:T(8,128)S(1)}, f32[18,18,127]{2,1,0:T(8,128)}, u32[]{:S(2)}) copy-start(f32[18,18,127]{2,1,0:T(8,128)} %get-tuple-element.147) | copy-start | bytes 493780
  317.0 9.3 %copy-start.49 = (f32[18,18,1]{2,1,0:T(8,128)S(1)}, f32[18,18,1]{2,1,0:T(8,128)}, u32[]{:S(2)}) copy-start(f32[18,18,1]{2,1,0:T(8,128)} %get-tuple-element.135) | copy-start | bytes 3892
  317.0 10.5 %copy-start.46 = (f32[18,18,1]{2,1,0:T(8,128)S(1)}, f32[18,18,1]{2,1,0:T(8,128)}, u32[]{:S(2)}) copy-start(f32[18,18,1]{2,1,0:T(8,128)} %get-tuple-element.107) | copy-start | bytes 3892
  321.7 14.6 %copy-start.7 = (f32[18,18,127]{2,1,0:T(8,128)S(1)}, f32[18,18,127]{2,1,0:T(8,128)}, u32[]{:S(2)}) copy-start(f32[18,18,127]{2,1,0:T(8,128)} %get-tuple-element.126) | copy-start | bytes 493780
  321.7 14.6 %copy-start.44 = (f32[18,18,1]{2,1,0:T(8,128)S(1)}, f32[18,18,1]{2,1,0:T(8,128)}, u32[]{:S(2)}) copy-start(f32[18,18,1]{2,1,0:T(8,128)} %get-tuple-element.104) | copy-start | bytes 3892
  323.7 3.8 %collective-permute-start.4 = (f32[3,1,18,128]{3,2,1,0:T(8,128)S(1)}, f32[3,1,18,128]{3,2,1,0:T(8,128)S(1)}, u32[]{:S(2)}, u32[]{:S(2)}) collective-permute-start(f32[3,1,18,128]{3,2,1,0:T(8,128)S(1)} %slice.611), channel_id=1, source_target_pairs={{0,8},{8,16},{16,24},{24,32},{32,40},{40,48},{48,56},{56,64},{64,7... | collective-permute-start | bytes 82952 | tf_op jit(solution)/shard_map/ppermute | solution.py:39
  327.4 7.6 %collective-permute-start.5 = (f32[3,1,18,128]{3,2,1,0:T(8,128)S(1)}, f32[3,1,18,128]{3,2,1,0:T(8,128)S(1)}, u32[]{:S(2)}, u32[]{:S(2)}) collective-permute-start(f32[3,1,18,128]{3,2,1,0:T(8,128)S(1)} %get-tuple-element.79), channel_id=1, source_target_pairs={{8,0},{16,8},{24,16},{32,24},{40,32},{48,40},{56,48},{64,56},{72,6... | collective-permute-start | bytes 82952 | tf_op jit(solution)/shard_map/ppermute | solution.py:40
  335.7 5.2 %collective-permute-start.6 = (f32[3,16,1,128]{3,2,1,0:T(1,128)S(1)}, f32[3,16,1,128]{3,2,1,0:T(1,128)S(1)}, u32[]{:S(2)}, u32[]{:S(2)}) collective-permute-start(f32[3,16,1,128]{3,2,1,0:T(1,128)S(1)} %get-tuple-element.78), channel_id=1, source_target_pairs={{0,1},{1,2},{2,3},{3,4},{4,5},{5,6},{6,7},{7,0},{8,9},{9,10},{10,1... | collective-permute-start | bytes 73736 | tf_op jit(solution)/shard_map/ppermute | solution.py:39
  337.9 4.8 %collective-permute-start.7 = (f32[3,16,1,128]{3,2,1,0:T(1,128)}, f32[3,16,1,128]{3,2,1,0:T(1,128)}, u32[]{:S(2)}, u32[]{:S(2)}) collective-permute-start(f32[3,16,1,128]{3,2,1,0:T(1,128)} %get-tuple-element.77), channel_id=1, source_target_pairs={{1,0},{2,1},{3,2},{4,3},{5,4},{6,5},{7,6},{0,7},{9,8},{10,9},{11,1... | collective-permute-start | bytes 73736 | tf_op jit(solution)/shard_map/ppermute | solution.py:40
  (54 other events, 180.3 us)
Sparse Core Ops, SparseCore 0:
  11.1 305.8 all-gather.1
where the time goes:
time: 367 us; the launch traced here: 365 us
  waiting for transfers between devices  224 us (61%)
  local copies, waits for them, and re-layouts  64 us (17%)
  other arithmetic  43.4 us (12%)
  between operations  15.3 us (4%)
  starting transfers between devices  11.1 us (3%)
  matrix products  7.67 us (2%)
    all_gather x1, waiting for transfers between devices, on_device(): lax.all_gather(panels, ('gx', 'gy'), axis=2, tiled=True)  205 us
    concatenate x26, local copies, waits for them, and re-layouts, on_device(): jnp.roll(widened[i, 1 - VELOCITY[i][0]:3 - VELOCITY[i][0] + cells_x, 1 -...  30.5 us
    ppermute x4, waiting for transfers between devices, extended(): after = lax.ppermute(first, axis, down)  13.2 us
    slice x6, local copies, waits for them, and re-layouts, on_device(): jnp.roll(widened[i, 1 - VELOCITY[i][0]:3 - VELOCITY[i][0] + cells_x, 1 -...  8.64 us
    unnamed x18, other arithmetic  8.58 us
    add x2, other arithmetic, moments(): total = total + fields[index]  7.64 us
    another operation x10, other arithmetic, on_device(): jnp.stack([jnp.roll(widened[i, 1 - VELOCITY[i][0]:3 - VELOCITY[i][0] + ce...  7.54 us
  transfers between devices with their start and end apart: 9, of which 7 were waited for; matrix products, arithmetic and copies ran while one was open for 24% of the time, Pallas kernels for 0%

commit v1 on v0

--- a/solution.py
+++ b/solution.py
@@ -124,7 +124,10 @@
     targets = jnp.einsum(
         "rcm,rmz->rcz",
         modal_vel,
-        lax.all_gather(panels, ("gx", "gy"), axis=2, tiled=True),
+        jnp.concatenate(
+            lax.all_to_all(jnp.stack([panels] * lax.axis_size(("gx", "gy"))), ("gx", "gy"), 0, 0),
+            axis=2,
+        ),
         preferred_element_type=jnp.float32,
     )
     pos_x = marker_x[0, 0]

time: 367 us -> 198 us (0.54)
  waiting for transfers between devices: 224 us -> 49.8 us
  between operations: 15.3 us -> 1.86 us
  starting transfers between devices: 11.1 us -> 23 us
  local copies, waits for them, and re-layouts: 64 us -> 73.5 us
    all_gather x1 -> x0, waiting for transfers between devices: 205 us -> none  [on_device(): lax.all_gather(panels, ('gx', 'gy'), axis=2, tiled=True)]
    ppermute x4, waiting for transfers between devices: 13.2 us -> 49.6 us  [extended(): after = lax.ppermute(first, axis, down)]
    all_to_all x0 -> x1, starting transfers between devices: none -> 10.5 us  [on_device(): lax.all_to_all(jnp.stack([panels] * lax.axis_size(('gx', 'gy'))), ('gx',...]
    all_to_all x0 -> x1, local copies, waits for them, and re-layouts: none -> 6.7 us  [on_device(): lax.all_to_all(jnp.stack([panels] * lax.axis_size(('gx', 'gy'))), ('gx',...]
    ppermute x4, waiting for transfers between devices: 6.17 us -> 0.26 us  [extended(): before = lax.ppermute(last, axis, up)]
  transfers between devices with their start and end apart: 9 -> 9, of which waited for: 7 -> 3; matrix products, arithmetic and copies ran while one was open for 24% -> 47% of each run, Pallas kernels for 0% -> 0%
where the time goes in v1:
time: 198 us; the launch traced here: 196 us
  local copies, waits for them, and re-layouts  73.5 us (37%)
  waiting for transfers between devices  49.8 us (25%)
  other arithmetic  41.8 us (21%)
  starting transfers between devices  23 us (12%)
  matrix products  6.07 us (3%)
    ppermute x4, waiting for transfers between devices, extended(): after = lax.ppermute(first, axis, down)  49.6 us
    concatenate x26, local copies, waits for them, and re-layouts, on_device(): jnp.roll(widened[i, 1 - VELOCITY[i][0]:3 - VELOCITY[i][0] + cells_x, 1 -...  30.2 us
    all_to_all x1, starting transfers between devices, on_device(): lax.all_to_all(jnp.stack([panels] * lax.axis_size(('gx', 'gy'))), ('gx',...  10.5 us
    another operation x10, other arithmetic, on_device(): jnp.stack([jnp.roll(widened[i, 1 - VELOCITY[i][0]:3 - VELOCITY[i][0] + ce...  8.12 us
    slice x6, local copies, waits for them, and re-layouts, on_device(): jnp.roll(widened[i, 1 - VELOCITY[i][0]:3 - VELOCITY[i][0] + cells_x, 1 -...  8.09 us
    add x2, other arithmetic, moments(): total = total + fields[index]  7.66 us
    add x3, other arithmetic, moments(): density = density + fields[index]  7.27 us
    ppermute x4, starting transfers between devices, extended(): after = lax.ppermute(first, axis, down)  7.16 us
  transfers between devices with their start and end apart: 9, of which 3 were waited for; matrix products, arithmetic and copies ran while one was open for 47% of the time, Pallas kernels for 0%

profile of v1, /device:TPU:97, one launch (start us, length us, event | category | flops | bytes accessed | tf_op | source)
XLA Modules:
  0.0 196.1 jit_solution(6225741025769865404)
XLA Ops:
  0.6 1.9 fusion.221
  2.5 1.9 collective-permute-start
  4.4 3.3 %stack.71 = bf16[128,64,200,1]{2,1,3,0:T(8,128)(2,1)} broadcast(bf16[64,200]{1,0:T(8,128)(2,1)} %bitcast.445), dimensions={1,2} | broadcast | bytes 3302400 | tf_op jit(solution)/shard_map/stack | solution.py:128
  7.8 10.5 %all-to-all-start = ((bf16[128,64,200,1]{2,1,3,0:T(8,128)(2,1)}), bf16[128,64,200,1]{2,1,3,0:T(8,128)(2,1)}, u32[]{:S(2)}, u32[]{:S(2)}) async-start(bf16[128,64,200,1]{2,1,3,0:T(8,128)(2,1)} %stack.71), calls=%async_computation | async-start | bytes 8388608 | tf_op jit(solution)/shard_map/all_to_all | solution.py:128
  18.5 2.0 %constant_dynamic-update-slice_fusion.1 = f32[19,20,16,128]{3,2,1,0:T(8,128)S(1)} fusion(f32[19,20,16,128]{3,2,1,0:T(8,128)S(1)} %constant_dynamic-update-slice_fusion.2, f32[19,16,16,128]{3,2,1,0:T(8,128)} %param.15), kind=kLoop, calls=%fused_computation.343 | loop fusion | bytes 4980736
  20.5 1.0 constant_dynamic-update-slice_fusion
  21.5 1.2 fusion.220
  22.7 3.5 %collective-permute-start.3 = (f32[19,20,2,128]{3,2,1,0:T(2,128)}, f32[19,20,2,128]{3,2,1,0:T(2,128)}, u32[]{:S(2)}, u32[]{:S(2)}) collective-permute-start(f32[19,20,2,128]{3,2,1,0:T(2,128)} %get-tuple-element.74), channel_id=1, source_target_pairs={{1,0},{2,1},{3,2},{4,3},{5,4},{6,5},{7,6},{0,7},{9,8},{10,9},{11,1... | collective-permute-start | bytes 1167368 | tf_op jit(solution)/shard_map/ppermute | solution.py:40
  26.2 1.0 broadcast_multiply_fusion
  27.2 2.1 %mul.602 = f32[512,324]{0,1:T(8,128)} reshape(f32[512,18,18]{0,2,1:T(8,128)} %broadcast_multiply_fusion) | data formatting | bytes 1327104 | tf_op jit(solution)/shard_map/mul | solution.py:144
  29.3 2.1 %mul.608 = f32[18,18,512]{2,1,0:T(8,128)} reshape(f32[324,512]{1,0:T(8,128)} %bitcast.443) | data formatting | bytes 1327104 | tf_op jit(solution)/shard_map/mul | solution.py:156
  32.0 42.8 %collective-permute-done.3 = f32[19,20,2,128]{3,2,1,0:T(2,128)} collective-permute-done((f32[19,20,2,128]{3,2,1,0:T(2,128)}, f32[19,20,2,128]{3,2,1,0:T(2,128)}, u32[]{:S(2)}, u32[]{:S(2)}) %collective-permute-start.3) | collective-permute-done | bytes 389152 | tf_op jit(solution)/shard_map/ppermute | solution.py:40
  75.6 1.0 slice_reduce_fusion
  76.7 0.9 slice_bitcast_fusion.16
  77.6 1.2 maximum_bitcast_fusion.8
  78.8 1.0 slice_bitcast_fusion.17
  79.8 1.0 slice_reduce_fusion.1
  80.8 1.0 slice_reduce_fusion.5
  81.8 1.1 slice_bitcast_fusion.21
  83.0 1.0 slice_bitcast_fusion.23
  83.9 1.7 slice_reduce_fusion.7
  86.4 1.5 slice_reduce_fusion.9
  87.9 0.9 concatenate.420
  88.8 1.8 concatenate.419
  90.5 0.9 concatenate.422
  91.4 1.8 concatenate.421
  94.0 0.9 concatenate.423
  94.9 1.8 concatenate.418
  96.7 0.9 concatenate.417
  97.6 1.8 concatenate.411
  99.3 1.8 concatenate.410
  101.1 1.8 concatenate.407
  102.8 1.8 concatenate.406
  104.7 2.9 %fusion.20 = (f32[18,18,128]{2,1,0:T(8,128)}, f32[1,18,18,128]{3,2,1,0:T(8,128)}, f32[1,18,18,128]{3,2,1,0:T(8,128)S(1)}, f32[1,18,18,128]{3,2,1,0:T(8,128)S(1)}...) fusion(f32[18,18,1]{2,1,0:T(8,128)} %get-tuple-element.141, f32[18,18,127]{2,1,0:T(8,128)} %get-tuple-element.151, ...), kind=kLoop, calls=%fused_computation.65 | loop fusion | flops 1161216 | bytes 5550080 | tf_op jit(solution)/shard_map/add | solution.py:58
  107.7 1.9 add_subtract_fusion
  111.9 1.8 slice_reduce_fusion.4
  113.7 0.9 concatenate.415
  114.6 0.9 concatenate.414
  115.5 1.8 concatenate.413
  117.3 0.9 concatenate.412
  118.2 0.9 concatenate.409
  119.1 0.9 concatenate.408
  120.0 0.9 concatenate.405
  120.8 1.8 stack.73
  122.6 2.8 %add_subtract_fusion.1 = f32[1,18,18,128]{3,2,1,0:T(8,128)} fusion(f32[1,18,18,128]{3,2,1,0:T(8,128)} %copy-done.32, f32[1,18,18,128]{3,2,1,0:T(8,128)} %copy-done.31, f32[1,18,18,128]{3,2,1,0:T(8,128)} %copy-done.30, f32[1,18,18,128]{3,2,1,0:T(8,128)} %copy-done.29, f32[19,20,2,128]{3,2,1,0:T(2,128)} %collective-permute-done.3, ...), kind=kLoop, calls=%fused_computation.74 | loop fusion | flops 705024 | bytes 5384192 | tf_op jit(solution)/shard_map/sub | solution.py:66
  125.5 1.8 stack.72
  127.2 4.0 %add_add_fusion = f32[1,18,18,128]{3,2,1,0:T(8,128)} fusion(f32[1,18,18,128]{3,2,1,0:T(8,128)} %copy-done.32, f32[1,18,18,128]{3,2,1,0:T(8,128)} %copy-done.31, f32[1,18,18,128]{3,2,1,0:T(8,128)} %copy-done.30, f32[1,18,18,128]{3,2,1,0:T(8,128)} %copy-done.29, f32[1,18,18,128]{3,2,1,0:T(8,128)} %get-tuple-element.57, ...), kind=kLoop, calls=%fused_computation.71 | loop fusion | flops 995328 | bytes 2654208 | tf_op jit(solution)/shard_map/add | solution.py:58
  131.3 1.6 div.77
  133.0 3.8 %subtract_add_fusion = f32[1,18,18,128]{3,2,1,0:T(8,128)} fusion(f32[1,18,18,1]{3,2,1,0:T(8,128)} %get-tuple-element.145, f32[1,18,18,127]{3,2,1,0:T(8,128)} %get-tuple-element.154, f32[1,18,18,127]{3,2,1,0:T(8,128)} %get-tuple-element.127, f32[1,18,18,1]{3,2,1,0:T(8,128)} %get-tuple-element.82, f32[1,18,18,127]{3,2,1,0:T(8,128)} %get-tuple-element.125, ...), kind=kLoop, calls=%fused_computation.72 | loop fusion | flops 787968 | bytes 1824768 | tf_op jit(solution)/shard_map/add | solution.py:64
  143.0 3.8 %fusion.27 = f32[1,324,128]{2,0,1:T(1,128)S(1)} fusion(f32[1,324,1]{2,0,1:T(1,128)S(1)} %copy-done.51, f32[1,324,127]{2,0,1:T(1,128)S(1)} %copy-done.52, f32[1,324,1]{2,0,1:T(1,128)S(1)} %copy-done.53, f32[1,324,127]{2,0,1:T(1,128)S(1)} %copy-done.54, f32[1,324,127]{2,0,1:T(1,128)S(1)} %copy-done.55, f32[1,324,1]{2,0,1:T(1,128)S(1)} %copy-done.56, ...), kind=kLoop, calls=%fused_computation.113 | loop fusion | flops 787968 | bytes 1824768 | tf_op jit(solution)/shard_map/add | solution.py:64
  147.4 1.1 multiply_reduce_fusion
  149.0 6.7 %copy.75 = bf16[128,64,200,1]{0,2,1,3:T(8,128)(2,1)} copy(bf16[128,64,200,1]{2,1,3,0:T(8,128)(2,1)} %all-to-all-done) | data formatting | bytes 6553600 | tf_op jit(solution)/shard_map/all_to_all | solution.py:128
  155.7 3.0 %fusion = f32[64,2,128]{2,1,0:T(2,128)S(1)} fusion(bf16[64,2,200]{2,1,0:T(2,128)(2,1)S(1)} %copy-done, bf16[128,64,200,1]{0,2,1,3:T(8,128)(2,1)} %copy.75), kind=kOutput, calls=%fused_computation | convolution fusion | flops 6553600 | bytes 3393536 | tf_op jit(solution)/shard_map/rcm,rmz->rcz/dot_general | solution.py:124
  159.2 1.5 fusion.2
  160.8 3.4 %collective-permute-start.4 = (f32[3,1,18,128]{3,2,1,0:T(8,128)S(1)}, f32[3,1,18,128]{3,2,1,0:T(8,128)S(1)}, u32[]{:S(2)}, u32[]{:S(2)}) collective-permute-start(f32[3,1,18,128]{3,2,1,0:T(8,128)S(1)} %slice.611), channel_id=1, source_target_pairs={{0,8},{8,16},{16,24},{24,32},{32,40},{40,48},{48,56},{56,64},{64,7... | collective-permute-start | bytes 82952 | tf_op jit(solution)/shard_map/ppermute | solution.py:39
  166.1 6.7 %collective-permute-done.5 = f32[3,1,18,128]{3,2,1,0:T(8,128)S(1)} collective-permute-done((f32[3,1,18,128]{3,2,1,0:T(8,128)S(1)}, f32[3,1,18,128]{3,2,1,0:T(8,128)S(1)}, u32[]{:S(2)}, u32[]{:S(2)}) %collective-permute-start.5) | collective-permute-done | bytes 27680 | tf_op jit(solution)/shard_map/ppermute | solution.py:40
  175.8 3.6 %collective-permute-start.7 = (f32[3,16,1,128]{3,2,1,0:T(1,128)}, f32[3,16,1,128]{3,2,1,0:T(1,128)}, u32[]{:S(2)}, u32[]{:S(2)}) collective-permute-start(f32[3,16,1,128]{3,2,1,0:T(1,128)} %get-tuple-element.77), channel_id=1, source_target_pairs={{1,0},{2,1},{3,2},{4,3},{5,4},{6,5},{7,6},{0,7},{9,8},{10,9},{11,1... | collective-permute-start | bytes 73736 | tf_op jit(solution)/shard_map/ppermute | solution.py:40
  179.4 1.7 scatter-add.16
  181.1 1.0 slice_add_fusion.2
  182.0 1.7 scatter-add.19
  183.7 2.3 %fusion.9 = (f32[3,16,16,128]{3,2,1,0:T(8,128)S(1)}, f32[3,16,16,128]{3,2,1,0:T(8,128)}) fusion(f32[1,18,18,128]{3,2,1,0:T(8,128)} %subtract_add_fusion, f32[1,18,18,128]{3,2,1,0:T(8,128)} %get-tuple-element.62, f32[1,18,18,128]{3,2,1,0:T(8,128)S(1)} %copy-done.42, f32[16,16,128]{2,1,0:T(8,128)S(1)} %fusion.191, f32[3,16,18,128]{3,2,1,0:T(8,128)} %scatter-add.19), kind=kLoop, calls=%fused_computation.14 | loop fusion | flops 491520 | bytes 1808384 | tf_op jit(solution)/shard_map/div | solution.py:72
  186.0 1.3 bitcast_dynamic-update-slice_fusion
  188.6 0.9 fusion.63
  194.6 1.4 copy-done.91
  (244 shorter events, 23.8 us)
Async XLA Ops:
  0.6 155.0 %copy-start = (bf16[64,2,200]{2,1,0:T(2,128)(2,1)S(1)}, bf16[64,2,200]{2,1,0:T(2,128)(2,1)}, u32[]{:S(2)}) copy-start(bf16[64,2,200]{2,1,0:T(2,128)(2,1)} %param.17) | copy-start | bytes 153604
  2.5 15.9 %collective-permute-start = (f32[19,2,16,128]{3,2,1,0:T(8,128)S(1)}, f32[19,2,16,128]{3,2,1,0:T(8,128)S(1)}, u32[]{:S(2)}, u32[]{:S(2)}) collective-permute-start(f32[19,2,16,128]{3,2,1,0:T(8,128)S(1)} %get-tuple-element.76), channel_id=1, source_target_pairs={{0,8},{8,16},{16,24},{24,32},{32,40},{40,48},{48,56},{56,64},{64,7... | collective-permute-start | bytes 933896 | tf_op jit(solution)/shard_map/ppermute | solution.py:39
  4.4 16.1 %collective-permute-start.1 = (f32[19,2,16,128]{3,2,1,0:T(8,128)}, f32[19,2,16,128]{3,2,1,0:T(8,128)}, u32[]{:S(2)}, u32[]{:S(2)}) collective-permute-start(f32[19,2,16,128]{3,2,1,0:T(8,128)} %get-tuple-element.75), channel_id=1, source_target_pairs={{8,0},{16,8},{24,16},{32,24},{40,32},{48,40},{56,48},{64,56},{72,6... | collective-permute-start | bytes 933896 | tf_op jit(solution)/shard_map/ppermute | solution.py:40
  7.8 10.6 %copy-start.89 = (s32[1,1,512]{2,1,0:T(1,128)S(1)}, s32[1,1,512]{2,1,0:T(1,128)}, u32[]{:S(2)}) copy-start(s32[1,1,512]{2,1,0:T(1,128)} %param.19) | copy-start | bytes 6148
  7.8 10.6 %copy-start.90 = (s32[1,1,512]{2,1,0:T(1,128)S(1)}, s32[1,1,512]{2,1,0:T(1,128)}, u32[]{:S(2)}) copy-start(s32[1,1,512]{2,1,0:T(1,128)} %param.18) | copy-start | bytes 6148
  7.8 141.2 %all-to-all-start = ((bf16[128,64,200,1]{2,1,3,0:T(8,128)(2,1)}), bf16[128,64,200,1]{2,1,3,0:T(8,128)(2,1)}, u32[]{:S(2)}, u32[]{:S(2)}) async-start(bf16[128,64,200,1]{2,1,3,0:T(8,128)(2,1)} %stack.71), calls=%async_computation | async-start | bytes 8388608 | tf_op jit(solution)/shard_map/all_to_all | solution.py:128
  21.5 9.9 %copy-start.92 = (s32[1,1,512]{2,1,0:T(1,128)S(1)}, s32[1,1,512]{2,1,0:T(1,128)}, u32[]{:S(2)}) copy-start(s32[1,1,512]{2,1,0:T(1,128)} %param.21) | copy-start | bytes 6148
  22.7 52.2 %collective-permute-start.3 = (f32[19,20,2,128]{3,2,1,0:T(2,128)}, f32[19,20,2,128]{3,2,1,0:T(2,128)}, u32[]{:S(2)}, u32[]{:S(2)}) collective-permute-start(f32[19,20,2,128]{3,2,1,0:T(2,128)} %get-tuple-element.74), channel_id=1, source_target_pairs={{1,0},{2,1},{3,2},{4,3},{5,4},{6,5},{7,6},{0,7},{9,8},{10,9},{11,1... | collective-permute-start | bytes 1167368 | tf_op jit(solution)/shard_map/ppermute | solution.py:40
  32.0 45.5 %collective-permute-start.2 = (f32[19,20,2,128]{3,2,1,0:T(2,128)}, f32[19,20,2,128]{3,2,1,0:T(2,128)S(1)}, u32[]{:S(2)}, u32[]{:S(2)}) collective-permute-start(f32[19,20,2,128]{3,2,1,0:T(2,128)} %get-tuple-element.73), channel_id=1, source_target_pairs={{0,1},{1,2},{2,3},{3,4},{4,5},{5,6},{6,7},{7,0},{8,9},{9,10},{10,1... | collective-permute-start | bytes 1167368 | tf_op jit(solution)/shard_map/ppermute | solution.py:39
  77.6 15.6 %copy-start.8 = (f32[18,18,127]{2,1,0:T(8,128)}, f32[18,18,127]{2,1,0:T(8,128)S(1)}, u32[]{:S(2)}) copy-start(f32[18,18,127]{2,1,0:T(8,128)S(1)} %get-tuple-element.126) | copy-start | bytes 493780
  109.6 8.5 %copy-start.86 = (f32[18,18]{1,0:T(8,128)S(1)}, f32[18,18]{1,0:T(8,128)}, u32[]{:S(2)}) copy-start(f32[18,18]{1,0:T(8,128)} %get-tuple-element.87) | copy-start | bytes 3892
  109.6 9.4 %copy-start.85 = (f32[18,18]{1,0:T(8,128)S(1)}, f32[18,18]{1,0:T(8,128)}, u32[]{:S(2)}) copy-start(f32[18,18]{1,0:T(8,128)} %get-tuple-element.146) | copy-start | bytes 3892
  109.7 10.3 %copy-start.87 = (f32[18,18]{1,0:T(8,128)S(1)}, f32[18,18]{1,0:T(8,128)}, u32[]{:S(2)}) copy-start(f32[18,18]{1,0:T(8,128)} %get-tuple-element.81) | copy-start | bytes 3892
  132.9 4.9 %copy-start.20 = (f32[18,18,127]{2,1,0:T(8,128)S(1)}, f32[18,18,127]{2,1,0:T(8,128)}, u32[]{:S(2)}) copy-start(f32[18,18,127]{2,1,0:T(8,128)} %get-tuple-element.153) | copy-start | bytes 493780
  132.9 4.9 %copy-start.47 = (f32[18,18,1]{2,1,0:T(8,128)S(1)}, f32[18,18,1]{2,1,0:T(8,128)}, u32[]{:S(2)}) copy-start(f32[18,18,1]{2,1,0:T(8,128)} %get-tuple-element.144) | copy-start | bytes 3892
  132.9 5.7 %copy-start.19 = (f32[18,18,127]{2,1,0:T(8,128)S(1)}, f32[18,18,127]{2,1,0:T(8,128)}, u32[]{:S(2)}) copy-start(f32[18,18,127]{2,1,0:T(8,128)} %get-tuple-element.112) | copy-start | bytes 493780
  132.9 5.7 %copy-start.46 = (f32[18,18,1]{2,1,0:T(8,128)S(1)}, f32[18,18,1]{2,1,0:T(8,128)}, u32[]{:S(2)}) copy-start(f32[18,18,1]{2,1,0:T(8,128)} %get-tuple-element.89) | copy-start | bytes 3892
  132.9 6.6 %copy-start.18 = (f32[18,18,127]{2,1,0:T(8,128)S(1)}, f32[18,18,127]{2,1,0:T(8,128)}, u32[]{:S(2)}) copy-start(f32[18,18,127]{2,1,0:T(8,128)} %get-tuple-element.151) | copy-start | bytes 493780
  132.9 6.5 %copy-start.45 = (f32[18,18,1]{2,1,0:T(8,128)S(1)}, f32[18,18,1]{2,1,0:T(8,128)}, u32[]{:S(2)}) copy-start(f32[18,18,1]{2,1,0:T(8,128)} %get-tuple-element.141) | copy-start | bytes 3892
  132.9 7.3 %copy-start.16 = (f32[18,18,127]{2,1,0:T(8,128)S(1)}, f32[18,18,127]{2,1,0:T(8,128)}, u32[]{:S(2)}) copy-start(f32[18,18,127]{2,1,0:T(8,128)} %get-tuple-element.116) | copy-start | bytes 493780
  132.9 7.3 %copy-start.41 = (f32[18,18,1]{2,1,0:T(8,128)S(1)}, f32[18,18,1]{2,1,0:T(8,128)}, u32[]{:S(2)}) copy-start(f32[18,18,1]{2,1,0:T(8,128)} %get-tuple-element.95) | copy-start | bytes 3892
  136.8 5.1 %copy-start.15 = (f32[18,18,127]{2,1,0:T(8,128)S(1)}, f32[18,18,127]{2,1,0:T(8,128)}, u32[]{:S(2)}) copy-start(f32[18,18,127]{2,1,0:T(8,128)} %get-tuple-element.149) | copy-start | bytes 493780
  136.8 5.1 %copy-start.40 = (f32[18,18,1]{2,1,0:T(8,128)S(1)}, f32[18,18,1]{2,1,0:T(8,128)}, u32[]{:S(2)}) copy-start(f32[18,18,1]{2,1,0:T(8,128)} %get-tuple-element.138) | copy-start | bytes 3892
  136.8 5.9 %copy-start.51 = (f32[1,324,1]{2,0,1:T(1,128)S(1)}, f32[1,324,1]{2,0,1:T(1,128)}, u32[]{:S(2)}) copy-start(f32[1,324,1]{2,0,1:T(1,128)} %concatenate.420) | copy-start | bytes 3892
  136.8 5.9 %copy-start.52 = (f32[1,324,127]{2,0,1:T(1,128)S(1)}, f32[1,324,127]{2,0,1:T(1,128)}, u32[]{:S(2)}) copy-start(f32[1,324,127]{2,0,1:T(1,128)} %concatenate.419) | copy-start | bytes 493780
  136.8 5.9 %copy-start.53 = (f32[1,324,1]{2,0,1:T(1,128)S(1)}, f32[1,324,1]{2,0,1:T(1,128)}, u32[]{:S(2)}) copy-start(f32[1,324,1]{2,0,1:T(1,128)} %concatenate.422) | copy-start | bytes 3892
  136.9 5.9 %copy-start.54 = (f32[1,324,127]{2,0,1:T(1,128)S(1)}, f32[1,324,127]{2,0,1:T(1,128)}, u32[]{:S(2)}) copy-start(f32[1,324,127]{2,0,1:T(1,128)} %concatenate.421) | copy-start | bytes 493780
  136.9 5.9 %copy-start.55 = (f32[1,324,127]{2,0,1:T(1,128)S(1)}, f32[1,324,127]{2,0,1:T(1,128)}, u32[]{:S(2)}) copy-start(f32[1,324,127]{2,0,1:T(1,128)} %concatenate.424) | copy-start | bytes 493780
  136.9 5.9 %copy-start.56 = (f32[1,324,1]{2,0,1:T(1,128)S(1)}, f32[1,324,1]{2,0,1:T(1,128)}, u32[]{:S(2)}) copy-start(f32[1,324,1]{2,0,1:T(1,128)} %concatenate.423) | copy-start | bytes 3892
  136.9 5.9 %copy-start.57 = (f32[1,324,127]{2,0,1:T(1,128)S(1)}, f32[1,324,127]{2,0,1:T(1,128)}, u32[]{:S(2)}) copy-start(f32[1,324,127]{2,0,1:T(1,128)} %concatenate.418) | copy-start | bytes 493780
  136.9 5.9 %copy-start.58 = (f32[1,324,1]{2,0,1:T(1,128)S(1)}, f32[1,324,1]{2,0,1:T(1,128)}, u32[]{:S(2)}) copy-start(f32[1,324,1]{2,0,1:T(1,128)} %concatenate.417) | copy-start | bytes 3892
  136.9 5.9 %copy-start.59 = (f32[1,324,127]{2,0,1:T(1,128)S(1)}, f32[1,324,127]{2,0,1:T(1,128)}, u32[]{:S(2)}) copy-start(f32[1,324,127]{2,0,1:T(1,128)} %concatenate.411) | copy-start | bytes 493780
  136.9 5.9 %copy-start.60 = (f32[1,324,127]{2,0,1:T(1,128)S(1)}, f32[1,324,127]{2,0,1:T(1,128)}, u32[]{:S(2)}) copy-start(f32[1,324,127]{2,0,1:T(1,128)} %concatenate.410) | copy-start | bytes 493780
  136.9 5.9 %copy-start.61 = (f32[1,324,127]{2,0,1:T(1,128)S(1)}, f32[1,324,127]{2,0,1:T(1,128)}, u32[]{:S(2)}) copy-start(f32[1,324,127]{2,0,1:T(1,128)} %concatenate.407) | copy-start | bytes 493780
  136.9 5.9 %copy-start.62 = (f32[1,324,127]{2,0,1:T(1,128)S(1)}, f32[1,324,127]{2,0,1:T(1,128)}, u32[]{:S(2)}) copy-start(f32[1,324,127]{2,0,1:T(1,128)} %concatenate.406) | copy-start | bytes 493780
  136.9 5.9 %copy-start.63 = (f32[1,324,127]{2,0,1:T(1,128)S(1)}, f32[1,324,127]{2,0,1:T(1,128)}, u32[]{:S(2)}) copy-start(f32[1,324,127]{2,0,1:T(1,128)} %concatenate.416) | copy-start | bytes 493780
  137.0 5.9 %copy-start.64 = (f32[1,324,1]{2,0,1:T(1,128)S(1)}, f32[1,324,1]{2,0,1:T(1,128)}, u32[]{:S(2)}) copy-start(f32[1,324,1]{2,0,1:T(1,128)} %concatenate.415) | copy-start | bytes 3892
  137.0 5.9 %copy-start.65 = (f32[1,324,1]{2,0,1:T(1,128)S(1)}, f32[1,324,1]{2,0,1:T(1,128)}, u32[]{:S(2)}) copy-start(f32[1,324,1]{2,0,1:T(1,128)} %concatenate.414) | copy-start | bytes 3892
  137.0 5.9 %copy-start.66 = (f32[1,324,127]{2,0,1:T(1,128)S(1)}, f32[1,324,127]{2,0,1:T(1,128)}, u32[]{:S(2)}) copy-start(f32[1,324,127]{2,0,1:T(1,128)} %concatenate.413) | copy-start | bytes 493780
  137.0 5.9 %copy-start.67 = (f32[1,324,1]{2,0,1:T(1,128)S(1)}, f32[1,324,1]{2,0,1:T(1,128)}, u32[]{:S(2)}) copy-start(f32[1,324,1]{2,0,1:T(1,128)} %concatenate.412) | copy-start | bytes 3892
  137.0 5.9 %copy-start.68 = (f32[1,324,1]{2,0,1:T(1,128)S(1)}, f32[1,324,1]{2,0,1:T(1,128)}, u32[]{:S(2)}) copy-start(f32[1,324,1]{2,0,1:T(1,128)} %concatenate.409) | copy-start | bytes 3892
  141.1 5.8 %copy-start.50 = (f32[324,128]{1,0:T(8,128)S(1)}, f32[324,128]{1,0:T(8,128)}, u32[]{:S(2)}) copy-start(f32[324,128]{1,0:T(8,128)} %div.77) | copy-start | bytes 497668
  141.1 5.8 %copy-start.71 = (f32[1,324,128]{2,0,1:T(1,128)S(1)}, f32[1,324,128]{2,0,1:T(1,128)}, u32[]{:S(2)}) copy-start(f32[1,324,128]{2,0,1:T(1,128)} %stack.73) | copy-start | bytes 497668
  141.1 5.8 %copy-start.72 = (f32[1,324,128]{2,0,1:T(1,128)S(1)}, f32[1,324,128]{2,0,1:T(1,128)}, u32[]{:S(2)}) copy-start(f32[1,324,128]{2,0,1:T(1,128)} %stack.72) | copy-start | bytes 497668
  142.9 4.5 %copy-start.6 = (f32[512,324]{0,1:T(8,128)S(1)}, f32[512,324]{0,1:T(8,128)}, u32[]{:S(2)}) copy-start(f32[512,324]{0,1:T(8,128)} %mul.602) | copy-start | bytes 1990660
  142.9 4.5 %copy-start.88 = (s32[1,1,512]{2,1,0:T(1,128)S(1)}, s32[1,1,512]{2,1,0:T(1,128)}, u32[]{:S(2)}) copy-start(s32[1,1,512]{2,1,0:T(1,128)} %param.20) | copy-start | bytes 6148
  142.9 5.6 %copy-start.9 = (f32[18,18,127]{2,1,0:T(8,128)S(1)}, f32[18,18,127]{2,1,0:T(8,128)}, u32[]{:S(2)}) copy-start(f32[18,18,127]{2,1,0:T(8,128)} %copy-done.8) | copy-start | bytes 493780
  143.0 5.6 %copy-start.11 = (f32[18,18,127]{2,1,0:T(8,128)S(1)}, f32[18,18,127]{2,1,0:T(8,128)}, u32[]{:S(2)}) copy-start(f32[18,18,127]{2,1,0:T(8,128)} %get-tuple-element.147) | copy-start | bytes 493780
  143.0 5.6 %copy-start.13 = (f32[18,18,127]{2,1,0:T(8,128)S(1)}, f32[18,18,127]{2,1,0:T(8,128)}, u32[]{:S(2)}) copy-start(f32[18,18,127]{2,1,0:T(8,128)} %get-tuple-element.124) | copy-start | bytes 493780
  143.0 5.6 %copy-start.34 = (f32[18,18,1]{2,1,0:T(8,128)S(1)}, f32[18,18,1]{2,1,0:T(8,128)}, u32[]{:S(2)}) copy-start(f32[18,18,1]{2,1,0:T(8,128)} %get-tuple-element.104) | copy-start | bytes 3892
  143.0 5.6 %copy-start.36 = (f32[18,18,1]{2,1,0:T(8,128)S(1)}, f32[18,18,1]{2,1,0:T(8,128)}, u32[]{:S(2)}) copy-start(f32[18,18,1]{2,1,0:T(8,128)} %get-tuple-element.135) | copy-start | bytes 3892
  143.0 5.6 %copy-start.38 = (f32[18,18,1]{2,1,0:T(8,128)S(1)}, f32[18,18,1]{2,1,0:T(8,128)}, u32[]{:S(2)}) copy-start(f32[18,18,1]{2,1,0:T(8,128)} %get-tuple-element.107) | copy-start | bytes 3892
  143.0 5.6 %copy-start.83 = (f32[18,18,128]{2,1,0:T(8,128)S(1)}, f32[18,18,128]{2,1,0:T(8,128)}, u32[]{:S(2)}) copy-start(f32[18,18,128]{2,1,0:T(8,128)} %get-tuple-element.56) | copy-start | bytes 497668
  155.7 8.4 %copy-start.12 = (f32[18,18,127]{2,1,0:T(8,128)S(1)}, f32[18,18,127]{2,1,0:T(8,128)}, u32[]{:S(2)}) copy-start(f32[18,18,127]{2,1,0:T(8,128)} %get-tuple-element.147) | copy-start | bytes 493780
  155.7 8.4 %copy-start.37 = (f32[18,18,1]{2,1,0:T(8,128)S(1)}, f32[18,18,1]{2,1,0:T(8,128)}, u32[]{:S(2)}) copy-start(f32[18,18,1]{2,1,0:T(8,128)} %get-tuple-element.135) | copy-start | bytes 3892
  155.7 9.6 %copy-start.14 = (f32[18,18,127]{2,1,0:T(8,128)S(1)}, f32[18,18,127]{2,1,0:T(8,128)}, u32[]{:S(2)}) copy-start(f32[18,18,127]{2,1,0:T(8,128)} %get-tuple-element.124) | copy-start | bytes 493780
  155.7 9.6 %copy-start.39 = (f32[18,18,1]{2,1,0:T(8,128)S(1)}, f32[18,18,1]{2,1,0:T(8,128)}, u32[]{:S(2)}) copy-start(f32[18,18,1]{2,1,0:T(8,128)} %get-tuple-element.107) | copy-start | bytes 3892
  158.8 14.7 %copy-start.10 = (f32[18,18,127]{2,1,0:T(8,128)S(1)}, f32[18,18,127]{2,1,0:T(8,128)}, u32[]{:S(2)}) copy-start(f32[18,18,127]{2,1,0:T(8,128)} %copy-done.8) | copy-start | bytes 493780
  158.8 14.7 %copy-start.35 = (f32[18,18,1]{2,1,0:T(8,128)S(1)}, f32[18,18,1]{2,1,0:T(8,128)}, u32[]{:S(2)}) copy-start(f32[18,18,1]{2,1,0:T(8,128)} %get-tuple-element.104) | copy-start | bytes 3892
  159.2 24.5 %copy-start.42 = (f32[1,18,18,128]{3,2,1,0:T(8,128)S(1)}, f32[1,18,18,128]{3,2,1,0:T(8,128)}, u32[]{:S(2)}) copy-start(f32[1,18,18,128]{3,2,1,0:T(8,128)} %add_subtract_fusion.1) | copy-start | bytes 497668
  160.8 4.4 %collective-permute-start.4 = (f32[3,1,18,128]{3,2,1,0:T(8,128)S(1)}, f32[3,1,18,128]{3,2,1,0:T(8,128)S(1)}, u32[]{:S(2)}, u32[]{:S(2)}) collective-permute-start(f32[3,1,18,128]{3,2,1,0:T(8,128)S(1)} %slice.611), channel_id=1, source_target_pairs={{0,8},{8,16},{16,24},{24,32},{32,40},{40,48},{48,56},{56,64},{64,7... | collective-permute-start | bytes 82952 | tf_op jit(solution)/shard_map/ppermute | solution.py:39
  165.2 7.6 %collective-permute-start.5 = (f32[3,1,18,128]{3,2,1,0:T(8,128)S(1)}, f32[3,1,18,128]{3,2,1,0:T(8,128)S(1)}, u32[]{:S(2)}, u32[]{:S(2)}) collective-permute-start(f32[3,1,18,128]{3,2,1,0:T(8,128)S(1)} %get-tuple-element.79), channel_id=1, source_target_pairs={{8,0},{16,8},{24,16},{32,24},{40,32},{48,40},{56,48},{64,56},{72,6... | collective-permute-start | bytes 82952 | tf_op jit(solution)/shard_map/ppermute | solution.py:40
  173.5 5.8 %collective-permute-start.6 = (f32[3,16,1,128]{3,2,1,0:T(1,128)S(1)}, f32[3,16,1,128]{3,2,1,0:T(1,128)S(1)}, u32[]{:S(2)}, u32[]{:S(2)}) collective-permute-start(f32[3,16,1,128]{3,2,1,0:T(1,128)S(1)} %get-tuple-element.78), channel_id=1, source_target_pairs={{0,1},{1,2},{2,3},{3,4},{4,5},{5,6},{6,7},{7,0},{8,9},{9,10},{10,1... | collective-permute-start | bytes 73736 | tf_op jit(solution)/shard_map/ppermute | solution.py:39
  175.8 5.3 %collective-permute-start.7 = (f32[3,16,1,128]{3,2,1,0:T(1,128)}, f32[3,16,1,128]{3,2,1,0:T(1,128)}, u32[]{:S(2)}, u32[]{:S(2)}) collective-permute-start(f32[3,16,1,128]{3,2,1,0:T(1,128)} %get-tuple-element.77), channel_id=1, source_target_pairs={{1,0},{2,1},{3,2},{4,3},{5,4},{6,5},{7,6},{0,7},{9,8},{10,9},{11,1... | collective-permute-start | bytes 73736 | tf_op jit(solution)/shard_map/ppermute | solution.py:40
  (38 other events, 90.2 us)
